TPU v7x, 256 devices: a whole 4x4x8 slice. The times are simulated.
256 devices in a mesh: view: 64 (over z, y, core), feat: 4 (over x).
Axes of the slice: x: 4, y: 4, z: 8, core: 2. Of those that a mesh axis runs over, the one named last changes fastest.
Arguments:
- points: bfloat16 [4096, 768, 128], P('view', 'feat'), may hold values from -6 to 6
- head_weight: bfloat16 [768, 768], P('feat'), may hold values from -0.21875 to 0.21875
- teacher: bfloat16 [768, 128, 1369], P('feat', 'view'), may hold values from -6 to 6
- splat_weight: bfloat16 [128, 64, 74, 128], P('view'), may hold values from 0 to 0.19921875
- block_owner: int32 [128, 16, 4], P('view'), may hold values from 0 to 63, all different within a row; in each aligned block of 32 rows (0 to 31, 32 to 63, ..., all dimensions but the last counted through in order) at most 3 rows name the same one
- block_local: int32 [128, 64], P('view'), may hold values from 0 to 63
- block_row: int32 [128, 64], P('view'), may hold values from 0 to 35, as said below
Outputs:
- grad_points: bfloat16 [4096, 768, 128], P('view', 'feat')
- head_grad: float32 [768, 768], P('feat')
Inputs may be any that keep to these rules, and one draw needn't show every extreme that they name: `block_owner`: over the 128 list entries of the views of one index of view, no owner appears more than 3 times, and some owner appears exactly 3 times. `block_row`: each view's list holds every value from 0 to 35 at least once.
All inputs are finite; a program needn't handle non-finite values.
Results may differ from a plain program's by a relative error of at most 0.0064.
Values may be sent and summed in bfloat16 or wider, within the bound.
A program may use at most 128 MiB of HBM per device.

v0:
```python
import jax
import jax.numpy as jnp
from jax import lax
from jax.sharding import PartitionSpec as P

GRID = 37
BAND = 2
BLOCK = 128


def slot_plan(owners, peer_count, capacity):
    total_requests = owners.shape[0]
    positions = jnp.arange(total_requests, dtype=jnp.int32)
    earlier = (owners[:, None] == owners[None, :]) & (positions[None, :] < positions[:, None])
    slot_rank = jnp.sum(earlier.astype(jnp.int32), axis=1)
    target = owners * capacity + slot_rank
    slot_ids = jnp.arange(peer_count * capacity, dtype=jnp.int32)
    matches = target[None, :] == slot_ids[:, None]
    source = jnp.sum(jnp.where(matches, positions[None, :], 0), axis=1)
    filled = jnp.any(matches, axis=1)
    return (target, source, filled)


def per_device(points, head_weight, teacher, splat_weight, block_owner, block_local, block_row):
    peer_count = lax.axis_size("view")
    local_width = points.shape[1]
    view_count = splat_weight.shape[0]
    visible = splat_weight.shape[1]
    requests = view_count * visible
    capacity = max(3, (3 * requests + 2 * peer_count - 1) // (2 * peer_count))
    owners = block_owner.reshape(requests)
    local_ids = block_local.reshape(requests)
    target, source, filled = slot_plan(owners, peer_count, capacity)
    wanted = jnp.where(filled, jnp.take(local_ids, source), 0)
    columns = jnp.arange(GRID, dtype=jnp.int32)
    row_masks = [
        (block_row[:, :, None] + offset == columns[None, None, :]).astype(jnp.bfloat16)
        for offset in range(BAND)
    ]
    empty_bf = jnp.zeros((), jnp.bfloat16)
    asked_ids = lax.all_to_all(wanted, "view", split_axis=0, concat_axis=0, tiled=True)
    sent_rows = jnp.take(points, asked_ids, axis=0)
    arrived = lax.all_to_all(sent_rows, "view", split_axis=0, concat_axis=0, tiled=True)
    fetched = jnp.take(arrived, target, axis=0).reshape(view_count, visible, local_width, BLOCK)
    contrib = jnp.einsum(
        "vjcp,vjdp->vjcd", splat_weight, fetched, preferred_element_type=jnp.float32
    ).astype(jnp.bfloat16)
    rendered = jnp.zeros((view_count, GRID, GRID, local_width), jnp.float32)
    for offset in range(BAND):
        band_part = contrib[:, :, offset * GRID : (offset + 1) * GRID, :]
        rendered = rendered + jnp.einsum(
            "vjr,vjcd->vrcd", row_masks[offset], band_part, preferred_element_type=jnp.float32
        )
    rendered_rows = rendered.astype(jnp.bfloat16).reshape(view_count * GRID * GRID, local_width)
    pixel_rows = rendered_rows.shape[0]
    teacher_width = head_weight.shape[1]
    local_teacher = teacher.shape[0]
    contract_first = (((0,), (1,)), ((), ()))
    projected = lax.psum_scatter(
        lax.dot_general(
            head_weight, rendered_rows, contract_first, preferred_element_type=jnp.float32
        ),
        "feat",
        scatter_dimension=0,
        tiled=True,
    )
    square_sum = lax.psum(jnp.sum(projected * projected, axis=0), "feat")
    scale_rows = jnp.sqrt(square_sum / teacher_width + 1e-06)
    normed = projected / scale_rows[None, :]
    target_feat = teacher.reshape(local_teacher, pixel_rows).astype(jnp.float32)
    residual = normed - target_feat
    row_dot = lax.psum(jnp.sum(residual * normed, axis=0), "feat")
    grad_proj = (
        (residual - normed * (row_dot / teacher_width)[None, :]) / scale_rows[None, :]
    ).astype(jnp.bfloat16)
    shard_part = lax.all_gather(grad_proj, "feat", axis=0, tiled=True)
    grad_image = lax.dot_general(
        shard_part, head_weight, contract_first, preferred_element_type=jnp.float32
    )
    column_part = lax.dot_general(
        rendered_rows, shard_part, contract_first, preferred_element_type=jnp.float32
    )
    grad_head = column_part
    grad_image, grad_head = (grad_image, grad_head)
    head_grad = lax.psum(grad_head, "view") / (view_count * peer_count * GRID)
    grad_image = grad_image.astype(jnp.bfloat16).reshape(view_count, GRID, GRID, local_width)
    pieces = [
        jnp.einsum("vjr,vrcd->vjcd", row_mask, grad_image, preferred_element_type=jnp.float32)
        for row_mask in row_masks
    ]
    grad_contrib = jnp.concatenate(pieces, axis=2).astype(jnp.bfloat16)
    grad_block = jnp.einsum(
        "vjcp,vjcd->vjdp", splat_weight, grad_contrib, preferred_element_type=jnp.float32
    ).astype(jnp.bfloat16)
    grad_block = grad_block.reshape(requests, local_width, BLOCK)
    packed = jnp.where(filled[:, None, None], jnp.take(grad_block, source, axis=0), empty_bf)
    landed = lax.all_to_all(packed, "view", split_axis=0, concat_axis=0, tiled=True)
    summed = jax.ops.segment_sum(
        landed.astype(jnp.float32), asked_ids, num_segments=points.shape[0]
    )
    grad_points = summed.astype(jnp.bfloat16)
    return (grad_points, head_grad)


def solution(mesh):
    placed = (
        P("view", "feat", None),
        P("feat", None),
        P("feat", "view", None),
        P("view", None, None, None),
        P("view", None, None),
        P("view", None),
        P("view", None),
    )
    return jax.shard_map(
        per_device,
        mesh=mesh,
        in_specs=placed,
        out_specs=(P("view", "feat", None), P("feat", None)),
        check_vma=False,
    )
```

profile of v0, /device:TPU:1, one launch (start us, length us, event | category | flops | bytes accessed | tf_op | source)
XLA Modules:
  0.0 846.6 jit_solution(4426664382847408768)
XLA Ops:
  11.4 22.4 %all_to_all.19 = s32[64,3,1]{1,2,0:T(1,128)S(1)} all-to-all(s32[64,3,1]{1,2,0:T(1,128)S(1)} %bitcast.40), channel_id=1, replica_groups=mesh['view'=64,'feat'=4] {'view'}, dimensions={0} | all-to-all | bytes 1536 | tf_op jit(solution)/shard_map/all_to_all | solution.py:41
  35.4 9.7 %gather_fusion.1 = bf16[192,192,128]{2,1,0:T(8,128)(2,1)} fusion(bf16[64,192,128]{2,1,0:T(8,128)(2,1)S(1)} %copy-done, s32[1024]{0:T(1024)S(1)} %pad_clamp_fusion.1), kind=kCustom, calls=%fused_computation.1 | custom fusion | bytes 18875136 | tf_op jit(solution)/shard_map/jit(_take)/gather | solution.py:42
  45.1 8.2 broadcast_select_fusion
  53.3 5.9 all-to-all-start.1
  60.2 204.1 %all-to-all-done.1 = bf16[192,192,128]{2,1,0:T(8,128)(2,1)} async-done(((bf16[192,192,128]{2,1,0:T(8,128)(2,1)}), bf16[192,192,128]{2,1,0:T(8,128)(2,1)}, u32[]{:S(2)}, u32[]{:S(2)}) %all-to-all-start.1) | async-done | bytes 9437216 | tf_op jit(solution)/shard_map/all_to_all | solution.py:43
  264.3 7.7 gather_fusion.2
  272.0 9.3 %convert_bitcast_fusion = bf16[2,64,74,192]{3,2,1,0:T(8,128)(2,1)} fusion(bf16[2,64,192,128]{3,2,1,0:T(8,128)(2,1)} %bitcast.38, pred[2,64]{1,0:T(4,128)(4,1)S(1)} %compare_and_fusion.1, bf16[2,64,74,128]{3,1,2,0:T(8,128)(2,1)S(1)} %copy-done.5), kind=kOutput, calls=%fused_computation.13 | convolution fusion | flops 470532096 | bytes 12353664 | tf_op jit(solution)/shard_map/vjcp,vjdp->vjcd/dot_general | solution.py:45
  281.3 4.3 fusion.36
  287.9 4.5 convolution_bitcast_fusion
  292.5 9.0 %copy.57 = f32[768,2738]{1,0:T(8,128)} copy(f32[768,2738]{0,1:T(8,128)} %convolution_bitcast_fusion) | data formatting | bytes 16822272
  304.4 83.7 %reduce-scatter.4.cloned.1.call-done = f32[192,2738]{1,0:T(8,128)} async-done(((f32[768,2738]{1,0:T(8,128)}), f32[192,2738]{1,0:T(8,128)}) %reduce-scatter.4.cloned.1.call-update) | async-done | bytes 2102800 | tf_op jit(solution)/shard_map/reduce_scatter | solution.py:59
  388.2 3.4 copy.58
  393.8 11.2 %psum.21 = f32[2738]{0:T(1024)S(1)} all-reduce(f32[2738]{0:T(1024)S(1)} %multiply_reduce_fusion), channel_id=1, replica_groups=mesh['view'=64,'feat'=4] {'feat'}, use_global_device_ids=true, to_apply=%region_5.6 | all-reduce | flops 2738 | bytes 21904 | tf_op jit(solution)/shard_map/psum | solution.py:67
  406.9 11.3 %psum.22 = f32[2738]{0:T(1024)S(1)} all-reduce(f32[2738]{0:T(1024)S(1)} %multiply_reduce_fusion.1), channel_id=1, replica_groups=mesh['view'=64,'feat'=4] {'feat'}, use_global_device_ids=true, to_apply=%region_7.8 | all-reduce | flops 2738 | bytes 21904 | tf_op jit(solution)/shard_map/psum | solution.py:72
  421.3 58.4 %all-gather.2.cloned.1.call-done = bf16[768,2738]{1,0:T(8,128)(2,1)} async-done(((bf16[192,2738]{1,0:T(8,128)(2,1)}), bf16[768,2738]{1,0:T(8,128)(2,1)}) %all-gather.2.cloned.1.call-update) | async-done | bytes 4205584 | tf_op jit(solution)/shard_map/all_gather | solution.py:76
  488.3 7.4 fusion.5
  495.7 12.4 %gather_fusion.3 = bf16[192,192,128]{2,1,0:T(8,128)(2,1)} fusion(bf16[128,192,128]{2,1,0:T(8,128)(2,1)} %bitcast.37, s32[1024]{0:T(1024)S(1)} %pad_clamp_fusion.2), kind=kCustom, calls=%fused_computation.3 | custom fusion | bytes 18875136 | tf_op jit(solution)/shard_map/jit(_take)/gather | solution.py:96
  508.2 9.9 %select_select_fusion = bf16[192,192,128]{2,1,0:T(8,128)(2,1)} fusion(bf16[192,192,128]{2,1,0:T(8,128)(2,1)} %gather_fusion.3, pred[192]{0:T(512)(128)(4,1)S(1)} %compare_and_fusion.2, pred[192]{0:T(512)(128)(4,1)S(1)} %fusion.21), kind=kLoop, calls=%fused_computation.5 | loop fusion | flops 9437184 | bytes 18874752 | tf_op jit(solution)/shard_map/jit(_where)/select_n | solution.py:96
  518.1 11.2 %all-to-all-start.2 = ((bf16[192,192,128]{2,1,0:T(8,128)(2,1)}), bf16[192,192,128]{2,1,0:T(8,128)(2,1)}, u32[]{:S(2)}, u32[]{:S(2)}) async-start(bf16[192,192,128]{2,1,0:T(8,128)(2,1)} %select_select_fusion), calls=%async_computation.2 | async-start | bytes 18874368 | tf_op jit(solution)/shard_map/all_to_all | solution.py:97
  529.3 4.6 fusion.37
  533.9 235.7 %all-reduce.2.cloned.1.call-done = f32[192,768]{1,0:T(8,128)} async-done(((f32[192,768]{1,0:T(8,128)}), f32[192,768]{1,0:T(8,128)}) %all-reduce.2.cloned.1.call-update) | async-done | bytes 589840 | tf_op jit(solution)/shard_map/psum | solution.py:85
  771.5 12.4 %convert_element_type.45 = f32[192,192,128]{2,1,0:T(8,128)} convert(bf16[192,192,128]{2,1,0:T(8,128)(2,1)} %all-to-all-done.2) | non-fusion elementwise | flops 4718592 | bytes 28311552 | tf_op jit(solution)/shard_map/convert_element_type | solution.py:99
  787.3 47.5 %scatter_fusion = f32[64,192,128]{2,1,0:T(8,128)} fusion(f32[64,192,128]{2,1,0:T(8,128)} %broadcast_in_dim.79, s32[192]{0:T(256)S(1)} %reshape.232, f32[192,192,128]{2,1,0:T(8,128)} %convert_element_type.45), kind=kCustom, calls=%fused_computation.4 | custom fusion | flops 4718592 | bytes 56623872 | tf_op jit(solution)/shard_map/scatter-add | solution.py:98
  834.8 5.0 convert_element_type.46
  (78 shorter events, 32.9 us)
Async XLA Ops:
  7.2 28.2 %copy-start = (bf16[64,192,128]{2,1,0:T(8,128)(2,1)S(1)}, bf16[64,192,128]{2,1,0:T(8,128)(2,1)}, u32[]{:S(2)}) copy-start(bf16[64,192,128]{2,1,0:T(8,128)(2,1)} %param.7) | copy-start | bytes 9437188
  53.3 6.4 copy-start.9
  53.3 6.9 copy-start.10
  53.3 211.0 %all-to-all-start.1 = ((bf16[192,192,128]{2,1,0:T(8,128)(2,1)}), bf16[192,192,128]{2,1,0:T(8,128)(2,1)}, u32[]{:S(2)}, u32[]{:S(2)}) async-start(bf16[192,192,128]{2,1,0:T(8,128)(2,1)} %broadcast_select_fusion), calls=%async_computation.1 | async-start | bytes 18874368 | tf_op jit(solution)/shard_map/all_to_all | solution.py:43
  59.2 328.9 %reduce-scatter.4.cloned.1.call-start = ((), (), s32[]{:S(2)}) async-start(), calls=%async_computation.6 | async-start | bytes 10813440 | tf_op jit(solution)/shard_map/reduce_scatter | solution.py:59
  60.2 211.8 %copy-start.5 = (bf16[2,64,74,128]{3,1,2,0:T(8,128)(2,1)S(1)}, bf16[2,64,74,128]{3,1,2,0:T(8,128)(2,1)}, u32[]{:S(2)}) copy-start(bf16[2,64,74,128]{3,1,2,0:T(8,128)(2,1)} %param.10) | copy-start | bytes 7274500
  286.9 1.0 copy-start.8
  287.9 4.5 copy-start.3
  301.5 1.2 copy-start.7
  301.5 178.2 %all-gather.2.cloned.1.call-start = ((), (), s32[]{:S(2)}) async-start(), calls=%async_computation.4 | async-start | bytes 5406720 | tf_op jit(solution)/shard_map/all_gather | solution.py:76
  388.2 16.8 %copy-start.2 = (f32[192,2738]{1,0:T(8,128)S(1)}, f32[192,2738]{1,0:T(8,128)}, u32[]{:S(2)}) copy-start(f32[192,2738]{1,0:T(8,128)} %reduce-scatter.4.cloned.1.call-done) | copy-start | bytes 6308356
  486.6 1.7 copy-start.6
  518.0 11.2 %copy-start.4 = (bf16[2738,192]{1,0:T(8,128)(2,1)S(1)}, bf16[2738,192]{1,0:T(8,128)(2,1)}, u32[]{:S(2)}) copy-start(bf16[2738,192]{1,0:T(8,128)(2,1)} %copy-done.3) | copy-start | bytes 3154180
  518.1 253.5 %all-to-all-start.2 = ((bf16[192,192,128]{2,1,0:T(8,128)(2,1)}), bf16[192,192,128]{2,1,0:T(8,128)(2,1)}, u32[]{:S(2)}, u32[]{:S(2)}) async-start(bf16[192,192,128]{2,1,0:T(8,128)(2,1)} %select_select_fusion), calls=%async_computation.2 | async-start | bytes 18874368 | tf_op jit(solution)/shard_map/all_to_all | solution.py:97
  529.2 240.4 %all-reduce.2.cloned.1.call-start = ((), (), s32[]{:S(2)}) async-start(), calls=%async_computation.5 | async-start | bytes 1179648 | tf_op jit(solution)/shard_map/psum | solution.py:85
  787.3 52.5 %copy-start.1 = (bf16[64,192,128]{2,1,0:T(8,128)(2,1)S(1)}, bf16[64,192,128]{2,1,0:T(8,128)(2,1)}, u32[]{:S(2)}) copy-start(bf16[64,192,128]{2,1,0:T(8,128)(2,1)} %param.7) | copy-start | bytes 9437188
Sparse Core Ops, SparseCore 0:
  301.7 86.4 reduce-scatter.3
  421.4 58.2 all-gather.1
  534.1 235.4 all-reduce.1
where the time goes:
time: 853 us; the launch traced here: 847 us
  waiting for transfers between devices  582 us (68%)
  other arithmetic  94.1 us (11%)
  local copies, waits for them, and re-layouts  61.6 us (7%)
  blocking collectives  44.9 us (5%)
  matrix products  32.1 us (4%)
  starting transfers between devices  17.7 us (2%)
  between operations  14.3 us (2%)
    psum x1, waiting for transfers between devices, per_device(): head_grad = lax.psum(grad_head, 'view') / (view_count * peer_count * GRID)  236 us
    all_to_all x1, waiting for transfers between devices, per_device(): lax.all_to_all(sent_rows, 'view', split_axis=0, concat_axis=0, tiled=True)  204 us
    reduce_scatter x1, waiting for transfers between devices, per_device(): lax.psum_scatter(lax.dot_general(head_weight, rendered_rows, contract_fir...  83.7 us
    all_gather x1, waiting for transfers between devices, per_device(): shard_part = lax.all_gather(grad_proj, 'feat', axis=0, tiled=True)  58.4 us
    scatter-add x1, other arithmetic, per_device(): jax.ops.segment_sum(landed.astype(jnp.float32), asked_ids, num_segments=p...  47.5 us
    all_to_all x1, blocking collectives, per_device(): lax.all_to_all(wanted, 'view', split_axis=0, concat_axis=0, tiled=True)  22.4 us
  transfers between devices with their start and end apart: 5, of which 4 were waited for; matrix products, arithmetic and copies ran while one was open for 1% of the time, Pallas kernels for 0%

commit v1 on v0

--- a/solution.py
+++ b/solution.py
@@ -82,7 +82,9 @@
     )
     grad_head = column_part
     grad_image, grad_head = (grad_image, grad_head)
-    head_grad = lax.psum(grad_head, "view") / (view_count * peer_count * GRID)
+    head_grad = jnp.sum(lax.all_gather(grad_head, "view"), axis=0) / (
+        view_count * peer_count * GRID
+    )
     grad_image = grad_image.astype(jnp.bfloat16).reshape(view_count, GRID, GRID, local_width)
     pieces = [
         jnp.einsum("vjr,vrcd->vjcd", row_mask, grad_image, preferred_element_type=jnp.float32)

time: 853 us -> 934 us (1.095)
  blocking collectives: 44.9 us -> 361 us
  waiting for transfers between devices: 582 us -> 346 us
  starting transfers between devices: 17.7 us -> 6.42 us
  other arithmetic: 94.1 us -> 104 us
    all_to_all x0 -> x1, blocking collectives: none -> 307 us  [per_device(): lax.all_to_all(packed, 'view', split_axis=0, concat_axis=0, tiled=True)]
    psum x1 -> x0, waiting for transfers between devices: 236 us -> none  [per_device(): head_grad = lax.psum(grad_head, 'view') / (view_count * peer_count * GRID)]
    reduce_sum x0 -> x1, other arithmetic: none -> 14.5 us  [per_device(): jnp.sum(lax.all_gather(grad_head, 'view'), axis=0)]
    all_to_all x1 -> x0, starting transfers between devices: 11.2 us -> none  [per_device(): lax.all_to_all(packed, 'view', split_axis=0, concat_axis=0, tiled=True)]
  transfers between devices with their start and end apart: 5 -> 4, of which waited for: 4 -> 3; matrix products, arithmetic and copies ran while one was open for 1% -> 11% of each run, Pallas kernels for 0% -> 0%
where the time goes in v1:
time: 934 us; the launch traced here: 926 us
  blocking collectives  361 us (39%)
  waiting for transfers between devices  346 us (37%)
  other arithmetic  104 us (11%)
  local copies, waits for them, and re-layouts  61.7 us (7%)
  matrix products  32.4 us (3%)
  between operations  14.3 us (2%)
    all_to_all x1, blocking collectives, per_device(): lax.all_to_all(packed, 'view', split_axis=0, concat_axis=0, tiled=True)  307 us
    all_to_all x1, waiting for transfers between devices, per_device(): lax.all_to_all(sent_rows, 'view', split_axis=0, concat_axis=0, tiled=True)  204 us
    reduce_scatter x1, waiting for transfers between devices, per_device(): lax.psum_scatter(lax.dot_general(head_weight, rendered_rows, contract_fir...  83.7 us
    all_gather x1, waiting for transfers between devices, per_device(): shard_part = lax.all_gather(grad_proj, 'feat', axis=0, tiled=True)  58.4 us
    scatter-add x1, other arithmetic, per_device(): jax.ops.segment_sum(landed.astype(jnp.float32), asked_ids, num_segments=p...  47.1 us
    all_to_all x1, blocking collectives, per_device(): lax.all_to_all(wanted, 'view', split_axis=0, concat_axis=0, tiled=True)  22.4 us
    psum x1, blocking collectives, per_device(): row_dot = lax.psum(jnp.sum(residual * normed, axis=0), 'feat')  20.1 us
  transfers between devices with their start and end apart: 4, of which 3 were waited for; matrix products, arithmetic and copies ran while one was open for 11% of the time, Pallas kernels for 0%

profile of v1, /device:TPU:1, one launch (start us, length us, event | category | flops | bytes accessed | tf_op | source)
XLA Modules:
  0.0 926.3 jit_solution(1917710731818246718)
XLA Ops:
  11.4 22.4 %all_to_all.19 = s32[64,3,1]{1,2,0:T(1,128)S(1)} all-to-all(s32[64,3,1]{1,2,0:T(1,128)S(1)} %bitcast.42), channel_id=1, replica_groups=mesh['view'=64,'feat'=4] {'view'}, dimensions={0} | all-to-all | bytes 1536 | tf_op jit(solution)/shard_map/all_to_all | solution.py:41
  35.4 9.7 %gather_fusion.1 = bf16[192,192,128]{2,1,0:T(8,128)(2,1)} fusion(bf16[64,192,128]{2,1,0:T(8,128)(2,1)S(1)} %copy-done, s32[1024]{0:T(1024)S(1)} %pad_clamp_fusion.1), kind=kCustom, calls=%fused_computation.1 | custom fusion | bytes 18875136 | tf_op jit(solution)/shard_map/jit(_take)/gather | solution.py:42
  45.1 8.3 broadcast_select_fusion
  53.3 5.9 all-to-all-start.1
  60.1 204.2 %all-to-all-done.1 = bf16[192,192,128]{2,1,0:T(8,128)(2,1)} async-done(((bf16[192,192,128]{2,1,0:T(8,128)(2,1)}), bf16[192,192,128]{2,1,0:T(8,128)(2,1)}, u32[]{:S(2)}, u32[]{:S(2)}) %all-to-all-start.1) | async-done | bytes 9437216 | tf_op jit(solution)/shard_map/all_to_all | solution.py:43
  264.3 7.7 gather_fusion.2
  272.0 9.3 %convert_bitcast_fusion = bf16[2,64,74,192]{3,2,1,0:T(8,128)(2,1)} fusion(bf16[2,64,192,128]{3,2,1,0:T(8,128)(2,1)} %bitcast.40, pred[2,64]{1,0:T(4,128)(4,1)S(1)} %compare_and_fusion.1, bf16[2,64,74,128]{3,1,2,0:T(8,128)(2,1)S(1)} %copy-done.4), kind=kOutput, calls=%fused_computation.13 | convolution fusion | flops 470532096 | bytes 12353664 | tf_op jit(solution)/shard_map/vjcp,vjdp->vjcd/dot_general | solution.py:45
  281.3 4.3 fusion.36
  288.0 4.5 convolution_bitcast_fusion
  292.5 9.0 copy.57
  304.5 83.7 %reduce-scatter.4.cloned.1.call-done = f32[192,2738]{1,0:T(8,128)} async-done(((f32[768,2738]{1,0:T(8,128)}), f32[192,2738]{1,0:T(8,128)}) %reduce-scatter.4.cloned.1.call-update) | async-done | bytes 2102800 | tf_op jit(solution)/shard_map/reduce_scatter | solution.py:59
  388.2 3.4 copy.58
  393.8 11.2 %psum.14 = f32[2738]{0:T(1024)S(1)} all-reduce(f32[2738]{0:T(1024)S(1)} %multiply_reduce_fusion), channel_id=1, replica_groups=mesh['view'=64,'feat'=4] {'feat'}, use_global_device_ids=true, to_apply=%region_5.6 | all-reduce | flops 2738 | bytes 21904 | tf_op jit(solution)/shard_map/psum | solution.py:67
  406.9 20.1 %psum.15 = f32[2738]{0:T(1024)S(1)} all-reduce(f32[2738]{0:T(1024)S(1)} %multiply_reduce_fusion.1), channel_id=1, replica_groups=mesh['view'=64,'feat'=4] {'feat'}, use_global_device_ids=true, to_apply=%region_7.8 | all-reduce | flops 2738 | bytes 21904 | tf_op jit(solution)/shard_map/psum | solution.py:72
  430.1 58.4 %all-gather.4.cloned.1.call-done = bf16[768,2738]{1,0:T(8,128)(2,1)} async-done(((bf16[192,2738]{1,0:T(8,128)(2,1)}), bf16[768,2738]{1,0:T(8,128)(2,1)}) %all-gather.4.cloned.1.call-update) | async-done | bytes 4205584 | tf_op jit(solution)/shard_map/all_gather | solution.py:76
  488.5 5.1 fusion.37
  502.1 7.4 fusion.5
  509.5 12.5 %gather_fusion.3 = bf16[192,192,128]{2,1,0:T(8,128)(2,1)} fusion(bf16[128,192,128]{2,1,0:T(8,128)(2,1)} %bitcast.38, s32[1024]{0:T(1024)S(1)} %pad_clamp_fusion.2), kind=kCustom, calls=%fused_computation.3 | custom fusion | bytes 18875136 | tf_op jit(solution)/shard_map/jit(_take)/gather | solution.py:98
  522.0 5.9 select_select_fusion
  527.9 307.4 %all_to_all.20 = bf16[192,192,128]{2,1,0:T(8,128)(2,1)} all-to-all(bf16[192,192,128]{2,1,0:T(8,128)(2,1)S(1)} %select_select_fusion), channel_id=1, replica_groups=mesh['view'=64,'feat'=4] {'view'}, dimensions={0} | all-to-all | bytes 18874368 | tf_op jit(solution)/shard_map/all_to_all | solution.py:99
  835.4 12.2 %convert_element_type.45 = f32[192,192,128]{2,1,0:T(8,128)} convert(bf16[192,192,128]{2,1,0:T(8,128)(2,1)} %all_to_all.20) | non-fusion elementwise | flops 4718592 | bytes 28311552 | tf_op jit(solution)/shard_map/convert_element_type | solution.py:101
  850.9 47.1 %scatter_fusion = f32[64,192,128]{2,1,0:T(8,128)} fusion(f32[64,192,128]{2,1,0:T(8,128)} %broadcast_in_dim.79, s32[192]{0:T(256)S(1)} %reshape.232, f32[192,192,128]{2,1,0:T(8,128)} %convert_element_type.45), kind=kCustom, calls=%fused_computation.4 | custom fusion | flops 4718592 | bytes 56623872 | tf_op jit(solution)/shard_map/scatter-add | solution.py:100
  898.0 5.0 convert_element_type.46
  903.1 14.5 %reduce_sum.61 = f32[192,768]{1,0:T(8,128)} reduce(f32[64,192,768]{2,1,0:T(8,128)} %bitcast.39, f32[]{:T(128)} %constant.39.clone.1), dimensions={0}, to_apply=%region_9.10 | reduce | flops 9289728 | bytes 38338564 | tf_op jit(solution)/shard_map/reduce_sum | solution.py:85
  (76 shorter events, 32.8 us)
Async XLA Ops:
  7.2 28.2 %copy-start = (bf16[64,192,128]{2,1,0:T(8,128)(2,1)S(1)}, bf16[64,192,128]{2,1,0:T(8,128)(2,1)}, u32[]{:S(2)}) copy-start(bf16[64,192,128]{2,1,0:T(8,128)(2,1)} %param.7) | copy-start | bytes 9437188
  53.3 6.4 copy-start.8
  53.3 6.8 copy-start.9
  53.3 211.0 %all-to-all-start.1 = ((bf16[192,192,128]{2,1,0:T(8,128)(2,1)}), bf16[192,192,128]{2,1,0:T(8,128)(2,1)}, u32[]{:S(2)}, u32[]{:S(2)}) async-start(bf16[192,192,128]{2,1,0:T(8,128)(2,1)} %broadcast_select_fusion), calls=%async_computation.1 | async-start | bytes 18874368 | tf_op jit(solution)/shard_map/all_to_all | solution.py:43
  59.3 328.9 %reduce-scatter.4.cloned.1.call-start = ((), (), s32[]{:S(2)}) async-start(), calls=%async_computation.6 | async-start | bytes 10813440 | tf_op jit(solution)/shard_map/reduce_scatter | solution.py:59
  60.1 211.9 %copy-start.4 = (bf16[2,64,74,128]{3,1,2,0:T(8,128)(2,1)S(1)}, bf16[2,64,74,128]{3,1,2,0:T(8,128)(2,1)}, u32[]{:S(2)}) copy-start(bf16[2,64,74,128]{3,1,2,0:T(8,128)(2,1)} %param.10) | copy-start | bytes 7274500
  286.9 1.0 copy-start.7
  287.9 4.5 copy-start.3
  301.5 1.2 copy-start.6
  301.6 186.9 %all-gather.4.cloned.1.call-start = ((), (), s32[]{:S(2)}) async-start(), calls=%async_computation.4 | async-start | bytes 5406720 | tf_op jit(solution)/shard_map/all_gather | solution.py:76
  388.2 16.8 %copy-start.2 = (f32[192,2738]{1,0:T(8,128)S(1)}, f32[192,2738]{1,0:T(8,128)}, u32[]{:S(2)}) copy-start(f32[192,2738]{1,0:T(8,128)} %reduce-scatter.4.cloned.1.call-done) | copy-start | bytes 6308356
  430.0 473.0 %all-gather.6.cloned.1.call-start = ((), (), s32[]{:S(2)}) async-start(), calls=%async_computation.5 | async-start | bytes 38338560 | tf_op jit(solution)/shard_map/all_gather | solution.py:85
  500.4 1.7 copy-start.5
  903.1 16.4 %copy-start.1 = (bf16[64,192,128]{2,1,0:T(8,128)(2,1)S(1)}, bf16[64,192,128]{2,1,0:T(8,128)(2,1)}, u32[]{:S(2)}) copy-start(bf16[64,192,128]{2,1,0:T(8,128)(2,1)} %param.7) | copy-start | bytes 9437188
Sparse Core Ops, SparseCore 0:
  301.7 86.4 reduce-scatter.3
  430.2 58.2 all-gather.3
  493.7 340.6 all-gather.5
